TPU v7x, 32 devices: a whole 2x2x4 slice. The times are simulated.
32 devices in a mesh: rows: 16 (over z, x, core), dp: 2 (over y).
Axes of the slice: x: 2, y: 2, z: 4, core: 2. Of those that a mesh axis runs over, the one named last changes fastest.
Arguments:
- query_act: bfloat16 [128, 64, 128], P(('dp', 'rows')), parts along dimension 0, may hold values from -2.09375 to 2.09375
- key_act: bfloat16 [128, 64, 128], P(('dp', 'rows')), parts along dimension 0, may hold values from -2.09375 to 2.09375
- value_act: bfloat16 [128, 64, 128], P(('dp', 'rows')), parts along dimension 0, may hold values from -4 to 4
- attn_out: bfloat16 [128, 64, 128], P(('dp', 'rows')), parts along dimension 0, may hold values from -4 to 4
- grad_out: bfloat16 [128, 64, 128], P(('dp', 'rows')), parts along dimension 0, may hold values from -4 to 4
- pair_bias: bfloat16 [4, 128, 64], P(None, ('dp', 'rows')), parts along dimension 1, may hold values from -3 to 3
- log_norm: float32 [128, 4, 64], P(('dp', 'rows')), parts along dimension 0, may hold values from 6.8 to 8
- back_weight: bfloat16 [384, 128], replicated, may hold values from -2 to 2
Outputs:
- column_grad: bfloat16 [64, 128, 128], P('rows', 'dp'), parts along dimension 1
- bias_grad: float32 [4, 128, 64], P(None, ('dp', 'rows')), parts along dimension 1
There are 2 independent parts, one for each index of `dp`. A program takes and returns all parts, laid end to end along the dimension named above; an argument that names none is the same for every part. Nothing has to cross between parts.
All inputs are finite; a program needn't handle non-finite values.
Results may differ from a plain program's by a relative error of at most 0.008.
Values may be sent and summed in bfloat16 or wider, within the bound.
A program may use at most 64 MiB of HBM per device.

v0:
```python
import jax
import jax.numpy as jnp
from jax import lax
from jax.sharding import PartitionSpec as P


def query_block(activations, bias_block, offset, row_span):
    query_act, key_act, value_act, attn_out, grad_out, log_norm = activations
    row_count, length, feature_width = query_act.shape
    head_count = bias_block.shape[0]
    head_size = feature_width // head_count
    softmax_scale = head_size ** (-0.5)
    query_part = lax.dynamic_slice_in_dim(query_act, offset, row_span, 1).reshape(
        row_count, row_span, head_count, head_size
    )
    grad_part = lax.dynamic_slice_in_dim(grad_out, offset, row_span, 1).reshape(
        row_count, row_span, head_count, head_size
    )
    out_part = lax.dynamic_slice_in_dim(attn_out, offset, row_span, 1).reshape(
        row_count, row_span, head_count, head_size
    )
    norm_part = lax.dynamic_slice_in_dim(log_norm, offset, row_span, 2)
    key_heads = key_act.reshape(row_count, length, head_count, head_size)
    value_heads = value_act.reshape(row_count, length, head_count, head_size)
    scores = (
        jnp.einsum("ijhd,ikhd->ihjk", query_part, key_heads, preferred_element_type=jnp.float32)
        * softmax_scale
        + bias_block.astype(jnp.float32)[None]
    )
    probs = jnp.exp(scores - norm_part[:, :, :, None])
    probs_low = probs.astype(jnp.bfloat16)
    grad_value = jnp.einsum(
        "ihjk,ijhd->ikhd", probs_low, grad_part, preferred_element_type=jnp.float32
    )
    grad_prob = jnp.einsum(
        "ijhd,ikhd->ihjk", grad_part, value_heads, preferred_element_type=jnp.float32
    )
    row_delta = jnp.einsum(
        "ijhd,ijhd->ihj", grad_part.astype(jnp.float32), out_part.astype(jnp.float32)
    )
    grad_score = probs * (grad_prob - row_delta[:, :, :, None])
    score_low = grad_score.astype(jnp.bfloat16)
    grad_query = (
        jnp.einsum("ihjk,ikhd->ijhd", score_low, key_heads, preferred_element_type=jnp.float32)
        * softmax_scale
    )
    grad_key = (
        jnp.einsum("ihjk,ijhd->ikhd", score_low, query_part, preferred_element_type=jnp.float32)
        * softmax_scale
    )
    return (jnp.sum(grad_score, axis=0), grad_query, grad_key, grad_value)


def run_blocks(activations, bias_rows, offset, row_span):
    query_act = activations[0]
    row_count, length, feature_width = query_act.shape
    head_count = bias_rows.shape[0]
    head_size = feature_width // head_count
    block_width = 1
    for candidate in range(min(row_span, 128), 0, -1):
        if row_span % candidate == 0:
            block_width = candidate
            break
    if block_width == row_span:
        return query_block(activations, bias_rows, offset, row_span)

    def advance(block_index, totals):
        bias_total, query_total, key_total, value_total = totals
        inner = block_index * block_width
        bias_block = lax.dynamic_slice_in_dim(bias_rows, inner, block_width, 1)
        partial_value, grad_query, grad_key, grad_value = query_block(
            activations, bias_block, offset + inner, block_width
        )
        bias_total = lax.dynamic_update_slice_in_dim(bias_total, partial_value, inner, 1)
        query_total = lax.dynamic_update_slice_in_dim(query_total, grad_query, inner, 1)
        return (bias_total, query_total, key_total + grad_key, value_total + grad_value)

    start_totals = (
        jnp.zeros((head_count, row_span, length), jnp.float32),
        jnp.zeros((row_count, row_span, head_count, head_size), jnp.float32),
        jnp.zeros((row_count, length, head_count, head_size), jnp.float32),
        jnp.zeros((row_count, length, head_count, head_size), jnp.float32),
    )
    return lax.fori_loop(0, row_span // block_width, advance, start_totals)


def reduce_bias(partial_value):
    return lax.psum_scatter(partial_value, "rows", scatter_dimension=1, tiled=True)


def local(query_act, key_act, value_act, attn_out, grad_out, pair_bias, log_norm, back_weight):
    row_count, length, feature_width = query_act.shape
    head_count = pair_bias.shape[0]
    head_size = feature_width // head_count
    activations = (query_act, key_act, value_act, attn_out, grad_out, log_norm)
    grad_shape = (row_count, length, head_count, head_size)
    piece = jax.tree.map(lambda part: lax.all_gather(part, "rows", axis=1, tiled=True), pair_bias)
    anchor = jnp.int32(0)
    bias_total = jnp.zeros((head_count, length, length), jnp.float32)
    query_total = jnp.zeros(grad_shape, jnp.float32)
    key_total = jnp.zeros(grad_shape, jnp.float32)
    value_total = jnp.zeros(grad_shape, jnp.float32)
    piece_sum, query_piece, key_piece, value_piece = run_blocks(
        activations, piece, anchor, piece.shape[1]
    )
    bias_total = lax.dynamic_update_slice_in_dim(bias_total, piece_sum, anchor, 1)
    query_total = lax.dynamic_update_slice_in_dim(query_total, query_piece, anchor, 1)
    grad_key = key_total + key_piece
    grad_value = value_total + value_piece
    bias_grad = reduce_bias(bias_total)
    joined = jnp.concatenate(
        [
            query_total.reshape(row_count, length, feature_width),
            grad_key.reshape(row_count, length, feature_width),
            grad_value.reshape(row_count, length, feature_width),
        ],
        axis=2,
    ).astype(jnp.bfloat16)
    pair_rows = jnp.dot(joined, back_weight, preferred_element_type=jnp.float32).astype(
        jnp.bfloat16
    )
    swapped = jnp.transpose(pair_rows, (1, 0, 2))
    column_grad = lax.all_to_all(swapped, "rows", split_axis=0, concat_axis=1, tiled=True)
    return (column_grad, bias_grad)


def solution(mesh):
    return jax.shard_map(
        local,
        mesh=mesh,
        in_specs=(
            P(("dp", "rows"), None, None),
            P(("dp", "rows"), None, None),
            P(("dp", "rows"), None, None),
            P(("dp", "rows"), None, None),
            P(("dp", "rows"), None, None),
            P(None, ("dp", "rows"), None),
            P(("dp", "rows"), None, None),
            P(),
        ),
        out_specs=(P("rows", "dp", None), P(None, ("dp", "rows"), None)),
        check_vma=False,
    )
```

profile of v0, /device:TPU:0, one launch (start us, length us, event | category | flops | bytes accessed | tf_op | source)
XLA Modules:
  0.0 131.6 jit_solution(4514492444576305188)
XLA Ops:
  7.2 0.0 copy-start
  7.2 0.0 copy-start.1
  7.2 0.0 all-reduce.3.cloned.1.call-start
  7.2 1.0 copy.42
  8.2 0.0 copy-done.1
  8.2 0.0 copy-start.6
  8.3 0.1 copy.43
  8.4 0.5 copy-done.6
  8.9 23.2 %all_gather.3 = bf16[4,64,64]{2,0,1:T(4,128)(2,1)S(1)} all-gather(bf16[4,4,64]{2,0,1:T(4,128)(2,1)S(1)} %copy.44), channel_id=1, replica_groups=mesh['rows'=16,'dp'=2] {'rows'}, dimensions={1}, use_global_device_ids=true | all-gather | bytes 34816 | tf_op jit(solution)/shard_map/all_gather | solution.py:97
  32.2 0.0 copy-start.2
  32.2 0.8 copy-done.2
  33.0 0.0 copy-start.3
  33.0 0.1 copy.46
  33.2 0.7 copy-done.3
  33.9 0.0 copy-start.4
  33.9 0.1 copy.62
  34.0 0.7 copy-done.4
  34.7 0.1 copy.47
  34.8 0.0 copy-start.5
  34.8 0.1 fusion.7
  34.9 0.6 copy-done.5
  35.5 0.3 fusion.2
  35.9 1.0 fusion.18
  36.8 0.0 all-reduce.3.cloned.1.call-update
  36.9 0.2 fusion.4
  37.1 0.2 fusion.5
  37.3 0.2 convolution_convert_fusion
  37.5 0.1 copy.49
  37.6 0.1 copy.50
  37.7 0.1 copy.51
  37.8 0.0 copy-done
  37.9 0.2 fusion.6
  38.1 0.7 copy.52
  38.7 3.5 %all-to-all-start = ((bf16[64,4,128]{2,1,0:T(4,128)(2,1)}), bf16[64,4,128]{2,1,0:T(4,128)(2,1)S(1)}, u32[]{:S(2)}, u32[]{:S(2)}) async-start(bf16[64,4,128]{2,1,0:T(4,128)(2,1)} %copy.52), calls=%async_computation | async-start | bytes 131072 | tf_op jit(solution)/shard_map/all_to_all | solution.py:123
  42.3 0.0 copy-start.7
  42.3 0.6 copy-done.7
  42.9 0.6 dynamic-slice
  44.2 78.7 %all-reduce.3.cloned.1.call-done = f32[4,64,64]{2,1,0:T(8,128)} async-done(((f32[4,64,64]{2,1,0:T(8,128)}), f32[4,64,64]{2,1,0:T(8,128)}) %all-reduce.3.cloned.1.call-update) | async-done | bytes 65552
  122.8 1.3 %constant_dynamic-slice_fusion = f32[4,4,64]{2,1,0:T(4,128)} fusion(f32[4,64,64]{2,1,0:T(8,128)} %all-reduce.3.cloned.1.call-done, u32[]{:T(128)S(6)} %multiply.2), kind=kLoop, calls=%fused_computation.25 | loop fusion | bytes 8196
  124.1 0.0 all-to-all-done
  124.1 0.7 copy.53
  (2 shorter events, 0.0 us)
Async XLA Ops:
  7.2 30.7 %copy-start = (bf16[384,128]{1,0:T(8,128)(2,1)S(1)}, bf16[384,128]{1,0:T(8,128)(2,1)}, u32[]{:S(2)}) copy-start(bf16[384,128]{1,0:T(8,128)(2,1)} %param.15) | copy-start | bytes 294916
  7.2 1.1 copy-start.1
  7.2 115.6 %all-reduce.3.cloned.1.call-start = ((), (), s32[]{:S(2)}) async-start(), calls=%async_computation.1 | async-start | bytes 262144
  8.2 0.7 copy-start.6
  32.2 0.8 copy-start.2
  33.0 0.8 copy-start.3
  33.9 0.8 copy-start.4
  34.8 0.7 copy-start.5
  38.7 85.4 %all-to-all-start = ((bf16[64,4,128]{2,1,0:T(4,128)(2,1)}), bf16[64,4,128]{2,1,0:T(4,128)(2,1)S(1)}, u32[]{:S(2)}, u32[]{:S(2)}) async-start(bf16[64,4,128]{2,1,0:T(4,128)(2,1)} %copy.52), calls=%async_computation | async-start | bytes 131072 | tf_op jit(solution)/shard_map/all_to_all | solution.py:123
  42.3 0.7 copy-start.7
Sparse Core Ops, SparseCore 0:
  37.0 85.7 all-reduce.2
where the time goes:
time: 133 us; the launch traced here: 132 us
  waiting for transfers between devices  78.7 us (59%)
  blocking collectives  23.2 us (17%)
  between operations  14.8 us (11%)
  local copies, waits for them, and re-layouts  9.15 us (7%)
  starting transfers between devices  3.54 us (3%)
  matrix products  2.12 us (2%)
    unnamed x2, waiting for transfers between devices  78.7 us
    all_gather x1, blocking collectives, local(): lax.all_gather(part, 'rows', axis=1, tiled=True)  23.2 us
    unnamed x24, local copies, waits for them, and re-layouts  7.49 us
    all_to_all x1, starting transfers between devices, local(): lax.all_to_all(swapped, 'rows', split_axis=0, concat_axis=1, tiled=True)  3.5 us
  transfers between devices with their start and end apart: 2, of which 1 were waited for; matrix products, arithmetic and copies ran while one was open for 3% of the time, Pallas kernels for 0%

commit v1 on v0

v1 whole, which is shorter than its diff:
```python
import functools

import jax
import jax.numpy as jnp
from jax import lax
from jax.experimental import pallas as pl
from jax.experimental.pallas import tpu as pltpu
from jax.sharding import PartitionSpec as P

MESH = pl.DeviceIdType.MESH
BLOCK = 64
UNROLL = 16
F32 = jnp.float32
BF16 = jnp.bfloat16


def repeat(count, body):
    if count <= UNROLL:
        for step in range(count):
            body(step)
    else:
        lax.fori_loop(0, count, lambda step, carry: (body(step), carry)[1], 0)


def block_of(length):
    for width in range(min(length, BLOCK), 0, -1):
        if length % width == 0:
            return width


def nt(left, right):
    return lax.dot_general(left, right, (((1,), (1,)), ((), ())), preferred_element_type=F32)


def tn(left, right):
    return lax.dot_general(left, right, (((0,), (0,)), ((), ())), preferred_element_type=F32)


def nn(left, right):
    return jnp.dot(left, right, preferred_element_type=F32)


def kernel(
    n,
    query_hbm, key_hbm, value_hbm, out_hbm, grad_hbm, bias_hbm, norm_hbm, weight_hbm,
    pair_out, bias_out,
    query, key, value, attn, grad, bias, norm, weight,
    factor_own, factor, part, part_in, probs_free, score_free,
    key_wide, norm_rows, joined, pair_send,
    in_sem, factor_sem, part_sem, pair_sem, own_sem,
):
    me = lax.axis_index("rows")
    rows, length, width = query.shape
    heads = bias.shape[0]
    own = bias.shape[1]
    size = width // heads
    scale = size ** (-0.5)
    block = block_of(length)
    chunks = length // block
    owners = block // own
    wide = heads * length

    loads = []
    for at, (source, target) in enumerate(
        (
            (bias_hbm, bias), (query_hbm, query), (key_hbm, key), (norm_hbm, norm),
            (grad_hbm, grad), (out_hbm, attn), (value_hbm, value), (weight_hbm, weight),
        )
    ):
        load = pltpu.make_async_copy(source, target, in_sem.at[at])
        load.start()
        loads.append(load)

    def peer(step):
        return lax.rem(me + step + 1, n)

    barrier = pltpu.get_barrier_semaphore()
    repeat(
        n - 1,
        lambda step: pl.semaphore_signal(
            barrier, inc=1, device_id={"rows": peer(step)}, device_id_type=MESH
        ),
    )

    loads[0].wait()
    own_factor = jnp.exp(
        jnp.concatenate([bias[h].astype(F32) for h in range(heads)], axis=1)
    )
    factor_own[...] = own_factor
    for load in loads[1:7]:
        load.wait()

    head_mask = (
        lax.broadcasted_iota(jnp.int32, (wide, width), 0) // length
        == lax.broadcasted_iota(jnp.int32, (wide, width), 1) // size
    )
    spread = (
        lax.broadcasted_iota(jnp.int32, (2 * width, wide), 0) % width // size
        == lax.broadcasted_iota(jnp.int32, (2 * width, wide), 1) // length
    ).astype(F32).astype(BF16)
    norm_spread = (
        lax.broadcasted_iota(jnp.int32, (3 * heads, wide), 0) % heads
        == lax.broadcasted_iota(jnp.int32, (3 * heads, wide), 1) // length
    ).astype(F32).astype(BF16)

    def widen(array):
        zero = jnp.zeros((wide, width), BF16)
        return jnp.where(head_mask, jnp.concatenate([array] * heads, axis=0), zero)

    def norm_terms(array):
        first = array.astype(BF16).astype(F32)
        second = (array - first).astype(BF16).astype(F32)
        third = array - first - second
        return jnp.concatenate([first, second, third], axis=0).astype(BF16)

    for i in range(rows):
        key_wide[i] = widen(key[i])
        if chunks > 1:
            same = (
                lax.broadcasted_iota(jnp.int32, (3 * heads, 3 * heads), 0)
                == lax.broadcasted_iota(jnp.int32, (3 * heads, 3 * heads), 1)
            ).astype(F32).astype(BF16)
            norm_rows[i] = tn(norm_terms(norm[i]), same)

    def free_part(chunk):
        at = chunk * block if chunks == 1 else pl.multiple_of(chunk * block, block)
        total = None
        for i in range(rows):
            span = pl.ds(at, block)
            grad_i = grad[i, span, :]
            product = grad_i.astype(F32) * attn[i, span, :].astype(F32)
            high = product.astype(BF16)
            low = (product - high.astype(F32)).astype(BF16)
            delta = nn(jnp.concatenate([high, low], axis=1), spread)
            if chunks == 1:
                norm_wide = tn(norm_terms(norm[i]), norm_spread)
            else:
                norm_wide = nn(norm_rows[i, span, :].astype(BF16), norm_spread)
            scores = nt(query[i, span, :], key_wide[i]) * scale
            probs = jnp.exp(scores - norm_wide)
            score = probs * (nt(grad_i, widen(value[i])) - delta)
            probs_free[i, span, :] = probs
            score_free[i, span, :] = score
            total = score if total is None else total + score
        part[pl.ds(chunk * owners, owners)] = total.reshape(owners, own, wide)

    repeat(chunks, free_part) if chunks == 1 else lax.fori_loop(
        0, chunks, lambda c, carry: (free_part(c), carry)[1], 0
    )
    factor[me] = own_factor

    pl.semaphore_wait(barrier, n - 1)

    def send_factor(step):
        pltpu.make_async_remote_copy(
            src_ref=factor_own, dst_ref=factor.at[me],
            send_sem=factor_sem.at[0], recv_sem=factor_sem.at[1],
            device_id={"rows": peer(step)}, device_id_type=MESH,
        ).start()

    def send_part(step):
        other = peer(step)
        pltpu.make_async_remote_copy(
            src_ref=part.at[other], dst_ref=part_in.at[me],
            send_sem=part_sem.at[0], recv_sem=part_sem.at[1],
            device_id={"rows": other}, device_id_type=MESH,
        ).start()

    def send_pair(step):
        other = peer(step)
        pltpu.make_async_remote_copy(
            src_ref=pair_send.at[:, other], dst_ref=pair_out.at[me],
            send_sem=pair_sem.at[0], recv_sem=pair_sem.at[1],
            device_id={"rows": other}, device_id_type=MESH,
        ).start()

    def all_of(ref, sem):
        view = ref.at[pl.ds(0, n - 1)]
        pltpu.make_async_copy(view, view, sem).wait()

    repeat(n - 1, send_factor)
    part_in[me] = part[me]
    loads[7].wait()
    all_of(factor, factor_sem.at[1])
    repeat(n - 1, send_part)

    def fold(array):
        folded = None
        for h in range(heads):
            keep = lax.broadcasted_iota(jnp.int32, (length, width), 1) // size == h
            piece = jnp.where(keep, array[h * length : (h + 1) * length], 0.0)
            folded = piece if folded is None else folded + piece
        return folded

    if chunks == 1:
        factor_all = factor[...].reshape(length, wide)
        pieces = []
        for i in range(rows):
            probs_low = (probs_free[i] * factor_all).astype(BF16)
            score_low = (score_free[i] * factor_all).astype(BF16)
            grad_query = nn(score_low, key_wide[i]) * scale
            grad_key = fold(tn(score_low, query[i])) * scale
            grad_value = fold(tn(probs_low, grad[i]))
            pieces.append(
                jnp.concatenate([grad_query, grad_key, grad_value], axis=1).astype(BF16)
            )
        for i in range(rows):
            pair = nn(pieces[i], weight[...]).astype(BF16)
            pair_send[i] = pair.reshape(n, own, weight.shape[1])
    else:
        for i in range(rows):
            joined[...] = jnp.zeros_like(joined)

            def advance(chunk, carry):
                span = pl.ds(pl.multiple_of(chunk * block, block), block)
                factor_part = factor[pl.ds(chunk * owners, owners)].reshape(block, wide)
                probs_low = (probs_free[i, span, :] * factor_part).astype(BF16)
                score_low = (score_free[i, span, :] * factor_part).astype(BF16)
                joined[0, span, :] = nn(score_low, key_wide[i]) * scale
                joined[1] += fold(tn(score_low, query[i, span, :]))
                joined[2] += fold(tn(probs_low, grad[i, span, :]))
                return carry

            lax.fori_loop(0, chunks, advance, 0)
            whole = jnp.concatenate(
                [joined[0], joined[1] * scale, joined[2]], axis=1
            ).astype(BF16)
            pair = nn(whole, weight[...]).astype(BF16)
            pair_send[i] = pair.reshape(n, own, weight.shape[1])

    keep_own = pltpu.make_async_copy(pair_send.at[:, me], pair_out.at[me], own_sem)
    keep_own.start()
    repeat(n - 1, send_pair)

    all_of(part_in, part_sem.at[1])
    total = jnp.sum(part_in[...], axis=0) * factor_own[...]
    for h in range(heads):
        bias_out[h] = total[:, h * length : (h + 1) * length]

    keep_own.wait()
    all_of(factor, factor_sem.at[0])
    all_of(part_in, part_sem.at[0])
    all_of(pair_out, pair_sem.at[0])
    all_of(pair_out, pair_sem.at[1])


def local(n, query_act, key_act, value_act, attn_out, grad_out, pair_bias, log_norm, back_weight):
    rows, length, width = query_act.shape
    heads, own, _ = pair_bias.shape
    channels = back_weight.shape[1]
    wide = heads * length
    chunked = length // block_of(length) > 1
    act = pltpu.VMEM((rows, length, width), BF16)
    anywhere = pl.BlockSpec(memory_space=pl.ANY)
    pairs, bias_grad = pl.pallas_call(
        functools.partial(kernel, n),
        out_shape=(
            jax.ShapeDtypeStruct((n, rows, own, channels), BF16),
            jax.ShapeDtypeStruct((heads, own, length), F32),
        ),
        in_specs=[anywhere] * 8,
        out_specs=(anywhere, pl.BlockSpec(memory_space=pltpu.VMEM)),
        scratch_shapes=[
            act, act, act, act, act,
            pltpu.VMEM(pair_bias.shape, BF16),
            pltpu.VMEM(log_norm.shape, F32),
            pltpu.VMEM(back_weight.shape, BF16),
            pltpu.VMEM((own, wide), F32),
            pltpu.VMEM((n, own, wide), F32),
            pltpu.VMEM((n, own, wide), F32),
            pltpu.VMEM((n, own, wide), F32),
            pltpu.VMEM((rows, length, wide), F32),
            pltpu.VMEM((rows, length, wide), F32),
            pltpu.VMEM((rows, wide, width), BF16),
            pltpu.VMEM((rows, length, 3 * heads) if chunked else (rows, 8, 3 * heads), F32),
            pltpu.VMEM((3, length, width) if chunked else (3, 8, 128), F32),
            pltpu.VMEM((rows, n, own, channels), BF16),
            pltpu.SemaphoreType.DMA((8,)),
            pltpu.SemaphoreType.DMA((2,)),
            pltpu.SemaphoreType.DMA((2,)),
            pltpu.SemaphoreType.DMA((2,)),
            pltpu.SemaphoreType.DMA,
        ],
        compiler_params=pltpu.CompilerParams(
            collective_id=0, has_side_effects=True, vmem_limit_bytes=67043328 - (2 << 20)
        ),
    )(query_act, key_act, value_act, attn_out, grad_out, pair_bias, log_norm, back_weight)
    column_grad = jnp.transpose(pairs, (2, 0, 1, 3)).reshape(own, n * rows, channels)
    return (column_grad, bias_grad)


def solution(mesh):
    rows = P(("dp", "rows"), None, None)
    return jax.shard_map(
        functools.partial(local, mesh.shape["rows"]),
        mesh=mesh,
        in_specs=(rows, rows, rows, rows, rows, P(None, ("dp", "rows"), None), rows, P()),
        out_specs=(P("rows", "dp", None), P(None, ("dp", "rows"), None)),
        check_vma=False,
    )
```

time: 133 us -> 19.2 us (0.14)
  waiting for transfers between devices: 78.7 us -> 0 us
  blocking collectives: 23.2 us -> 0 us
  Pallas kernels: 0 us -> 16.3 us
  between operations: 14.8 us -> 0.65 us
  local copies, waits for them, and re-layouts: 9.15 us -> 2.09 us
  starting transfers between devices: 3.54 us -> 0 us
  matrix products: 2.12 us -> 0 us
    unnamed x2 -> x0, waiting for transfers between devices: 78.7 us -> none
    all_gather x1 -> x0, blocking collectives: 23.2 us -> none  [local(): lax.all_gather(part, 'rows', axis=1, tiled=True)]
    pallas_call x0 -> x1, Pallas kernels: none -> 16.3 us  [local(): pl.pallas_call(functools.partial(kernel, n), out_shape=(jax.ShapeDtypeStr...]
    unnamed x24 -> x4, local copies, waits for them, and re-layouts: 7.49 us -> 2.09 us
    all_to_all x1 -> x0, starting transfers between devices: 3.5 us -> none  [local(): lax.all_to_all(swapped, 'rows', split_axis=0, concat_axis=1, tiled=True)]
    dot_general x6 -> x0, matrix products: 2.12 us -> none  [the longest x1 0.97 us: query_block(): jnp.einsum('ijhd,ikhd->ihjk', grad_part, value_heads, preferred_element_t...]
  transfers between devices with their start and end apart: 2 -> 0, of which waited for: 1 -> 0; matrix products, arithmetic and copies ran while one was open for 3% -> 0% of each run, Pallas kernels for 0% -> 0%
where the time goes in v1:
time: 19.2 us; the launch traced here: 19 us
  Pallas kernels  16.3 us (85%)
  local copies, waits for them, and re-layouts  2.09 us (11%)
  between operations  0.65 us (3%)
    pallas_call x1, Pallas kernels, local(): pl.pallas_call(functools.partial(kernel, n), out_shape=(jax.ShapeDtypeStr...  16.3 us
    unnamed x4, local copies, waits for them, and re-layouts  2.09 us

profile of v1, /device:TPU:0, one launch (start us, length us, event | category | flops | bytes accessed | tf_op | source)
XLA Modules:
  0.0 19.0 jit_solution(6127160593182373684)
XLA Ops:
  0.6 16.3 %shard_map.95 = (bf16[16,4,4,128]{3,2,1,0:T(4,128)(2,1)}, f32[4,4,64]{2,1,0:T(4,128)}) custom-call(bf16[4,64,128]{2,1,0:T(8,128)(2,1)} %query_hbm.1, bf16[4,64,128]{2,1,0:T(8,128)(2,1)} %key_hbm.1, bf16[4,64,128]{2,1,0:T(8,128)(2,1)} %value_hbm.1, bf16[4,64,128]{2,1,0:T(8,128)(2,1)} %out_hbm.1, bf16[4,64,128]{2,1,0:T(8,128)(2,1)} %grad_hbm.1, ...), custom_call_target="tpu_custom_call" | custom-call | tf_op jit(solution)/shard_map/pallas_call | solution.py:255
  16.9 0.0 copy-start
  16.9 1.5 %copy.10 = bf16[4,64,128]{2,1,0:T(8,128)(2,1)} copy(bf16[4,64,128]{2,0,1:T(4,128)(2,1)} %bitcast.3) | data formatting | bytes 131072
  18.4 0.0 copy-done
  18.4 0.6 %copy.12 = f32[4,4,64]{2,1,0:T(4,128)} copy(f32[4,4,64]{2,1,0:T(4,128)S(1)} %copy-done) | data formatting | bytes 8192
Async XLA Ops:
  16.9 1.5 %copy-start = (f32[4,4,64]{2,1,0:T(4,128)S(1)}, f32[4,4,64]{2,1,0:T(4,128)}, u32[]{:S(2)}) copy-start(f32[4,4,64]{2,1,0:T(4,128)} %get-tuple-element.11) | copy-start | bytes 12292

commit v2 on v1

--- a/solution.py
+++ b/solution.py
@@ -71,8 +71,12 @@
         load.start()
         loads.append(load)
 
+    upper = me * 2 // n
+    near = upper * me + (1 - upper) * (n - 1 - me)
+
     def peer(step):
-        return lax.rem(me + step + 1, n)
+        other = step + (step - near + n) // n
+        return upper * other + (1 - upper) * (n - 1 - other)
 
     barrier = pltpu.get_barrier_semaphore()
     repeat(
@@ -169,7 +173,7 @@
     def send_pair(step):
         other = peer(step)
         pltpu.make_async_remote_copy(
-            src_ref=pair_send.at[:, other], dst_ref=pair_out.at[me],
+            src_ref=pair_send.at[other], dst_ref=pair_out.at[me],
             send_sem=pair_sem.at[0], recv_sem=pair_sem.at[1],
             device_id={"rows": other}, device_id_type=MESH,
         ).start()
@@ -179,10 +183,10 @@
         pltpu.make_async_copy(view, view, sem).wait()
 
     repeat(n - 1, send_factor)
+    repeat(n - 1, send_part)
     part_in[me] = part[me]
     loads[7].wait()
     all_of(factor, factor_sem.at[1])
-    repeat(n - 1, send_part)
 
     def fold(array):
         folded = None
@@ -206,7 +210,7 @@
             )
         for i in range(rows):
             pair = nn(pieces[i], weight[...]).astype(BF16)
-            pair_send[i] = pair.reshape(n, own, weight.shape[1])
+            pair_send[:, i] = pair.reshape(n, own, weight.shape[1])
     else:
         for i in range(rows):
             joined[...] = jnp.zeros_like(joined)
@@ -226,9 +230,9 @@
                 [joined[0], joined[1] * scale, joined[2]], axis=1
             ).astype(BF16)
             pair = nn(whole, weight[...]).astype(BF16)
-            pair_send[i] = pair.reshape(n, own, weight.shape[1])
-
-    keep_own = pltpu.make_async_copy(pair_send.at[:, me], pair_out.at[me], own_sem)
+            pair_send[:, i] = pair.reshape(n, own, weight.shape[1])
+
+    keep_own = pltpu.make_async_copy(pair_send.at[me], pair_out.at[me], own_sem)
     keep_own.start()
     repeat(n - 1, send_pair)
 
@@ -255,11 +259,11 @@
     pairs, bias_grad = pl.pallas_call(
         functools.partial(kernel, n),
         out_shape=(
-            jax.ShapeDtypeStruct((n, rows, own, channels), BF16),
-            jax.ShapeDtypeStruct((heads, own, length), F32),
+            pltpu.VMEM((n, rows, own, channels), BF16),
+            pltpu.VMEM((heads, own, length), F32),
         ),
         in_specs=[anywhere] * 8,
-        out_specs=(anywhere, pl.BlockSpec(memory_space=pltpu.VMEM)),
+        out_specs=(pl.BlockSpec(memory_space=pltpu.VMEM), pl.BlockSpec(memory_space=pltpu.VMEM)),
         scratch_shapes=[
             act, act, act, act, act,
             pltpu.VMEM(pair_bias.shape, BF16),
@@ -274,7 +278,7 @@
             pltpu.VMEM((rows, wide, width), BF16),
             pltpu.VMEM((rows, length, 3 * heads) if chunked else (rows, 8, 3 * heads), F32),
             pltpu.VMEM((3, length, width) if chunked else (3, 8, 128), F32),
-            pltpu.VMEM((rows, n, own, channels), BF16),
+            pltpu.VMEM((n, rows, own, channels), BF16),
             pltpu.SemaphoreType.DMA((8,)),
             pltpu.SemaphoreType.DMA((2,)),
             pltpu.SemaphoreType.DMA((2,)),

time: 19.2 us -> 16.8 us (0.88)
  Pallas kernels: 16.3 us -> 14.7 us
  local copies, waits for them, and re-layouts: 2.09 us -> 1.24 us
    pallas_call x1, Pallas kernels: 16.3 us -> 14.7 us  [local(): pl.pallas_call(functools.partial(kernel, n), out_shape=(pltpu.VMEM((n, ro...]
    unnamed x4 -> x2, local copies, waits for them, and re-layouts: 2.09 us -> 1.24 us
where the time goes in v2:
time: 16.8 us; the launch traced here: 16.6 us
  Pallas kernels  14.7 us (88%)
  local copies, waits for them, and re-layouts  1.24 us (7%)
  between operations  0.64 us (4%)
    pallas_call x1, Pallas kernels, local(): pl.pallas_call(functools.partial(kernel, n), out_shape=(pltpu.VMEM((n, ro...  14.7 us
    unnamed x2, local copies, waits for them, and re-layouts  1.24 us

profile of v2, /device:TPU:0, one launch (start us, length us, event | category | flops | bytes accessed | tf_op | source)
XLA Modules:
  0.0 16.6 jit_solution(12467623858710976736)
XLA Ops:
  0.6 14.7 %shard_map.95 = (bf16[16,4,4,128]{3,2,1,0:T(4,128)(2,1)S(1)}, f32[4,4,64]{2,1,0:T(4,128)S(1)}) custom-call(bf16[4,64,128]{2,1,0:T(8,128)(2,1)} %query_hbm.1, bf16[4,64,128]{2,1,0:T(8,128)(2,1)} %key_hbm.1, bf16[4,64,128]{2,1,0:T(8,128)(2,1)} %value_hbm.1, bf16[4,64,128]{2,1,0:T(8,128)(2,1)} %out_hbm.1, bf16[4,64,128]{2,1,0:T(8,128)(2,1)} %grad_hbm.1, ...), custom_call_target="tpu_custom_call" | custom-call | tf_op jit(solution)/shard_map/pallas_call | solution.py:259
  15.4 0.6 %copy.10 = bf16[4,64,128]{2,1,0:T(8,128)(2,1)} copy(bf16[4,64,128]{2,0,1:T(4,128)(2,1)S(1)} %bitcast.3) | data formatting | bytes 131072
  16.0 0.6 %copy.12 = f32[4,4,64]{2,1,0:T(4,128)} copy(f32[4,4,64]{2,1,0:T(4,128)S(1)} %get-tuple-element.9) | data formatting | bytes 8192

commit v3 on v2

--- a/solution.py
+++ b/solution.py
@@ -238,14 +238,22 @@
 
     all_of(part_in, part_sem.at[1])
     total = jnp.sum(part_in[...], axis=0) * factor_own[...]
-    for h in range(heads):
-        bias_out[h] = total[:, h * length : (h + 1) * length]
+    bias_out[...] = total
 
     keep_own.wait()
     all_of(factor, factor_sem.at[0])
     all_of(part_in, part_sem.at[0])
     all_of(pair_out, pair_sem.at[0])
     all_of(pair_out, pair_sem.at[1])
+
+
+def finish(pairs, total, column_out, bias_out):
+    n, rows, own, channels = pairs.shape
+    heads, _, length = bias_out.shape
+    landed = pairs[...].astype(F32).reshape(n * rows, own, channels)
+    column_out[...] = jnp.transpose(landed, (1, 0, 2)).astype(BF16)
+    for h in range(heads):
+        bias_out[h] = total[:, h * length : (h + 1) * length]
 
 
 def local(n, query_act, key_act, value_act, attn_out, grad_out, pair_bias, log_norm, back_weight):
@@ -260,7 +268,7 @@
         functools.partial(kernel, n),
         out_shape=(
             pltpu.VMEM((n, rows, own, channels), BF16),
-            pltpu.VMEM((heads, own, length), F32),
+            pltpu.VMEM((own, wide), F32),
         ),
         in_specs=[anywhere] * 8,
         out_specs=(pl.BlockSpec(memory_space=pltpu.VMEM), pl.BlockSpec(memory_space=pltpu.VMEM)),
@@ -289,8 +297,19 @@
             collective_id=0, has_side_effects=True, vmem_limit_bytes=67043328 - (2 << 20)
         ),
     )(query_act, key_act, value_act, attn_out, grad_out, pair_bias, log_norm, back_weight)
-    column_grad = jnp.transpose(pairs, (2, 0, 1, 3)).reshape(own, n * rows, channels)
-    return (column_grad, bias_grad)
+    vmem = pl.BlockSpec(memory_space=pltpu.VMEM)
+    return pl.pallas_call(
+        finish,
+        out_shape=(
+            jax.ShapeDtypeStruct((own, n * rows, channels), BF16),
+            jax.ShapeDtypeStruct((heads, own, length), F32),
+        ),
+        in_specs=[vmem, vmem],
+        out_specs=(vmem, vmem),
+    )(
+        pltpu.with_memory_space_constraint(pairs, pltpu.VMEM),
+        pltpu.with_memory_space_constraint(bias_grad, pltpu.VMEM),
+    )
 
 
 def solution(mesh):

time: 16.8 us -> 16.2 us (0.964)
  local copies, waits for them, and re-layouts: 1.24 us -> 0 us
  Pallas kernels: 14.7 us -> 15.4 us
    unnamed x2 -> x0, local copies, waits for them, and re-layouts: 1.24 us -> none
    pallas_call x0 -> x1, Pallas kernels: none -> 0.67 us  [local(): pl.pallas_call(finish, out_shape=(jax.ShapeDtypeStruct((own, n * rows, ch...]
where the time goes in v3:
time: 16.2 us; the launch traced here: 16.1 us
  Pallas kernels  15.4 us (95%)
  between operations  0.64 us (4%)
    pallas_call x1, Pallas kernels, local(): pl.pallas_call(functools.partial(kernel, n), out_shape=(pltpu.VMEM((n, ro...  14.7 us
    pallas_call x1, Pallas kernels, local(): pl.pallas_call(finish, out_shape=(jax.ShapeDtypeStruct((own, n * rows, ch...  0.67 us

profile of v3, /device:TPU:0, one launch (start us, length us, event | category | flops | bytes accessed | tf_op | source)
XLA Modules:
  0.0 16.1 jit_solution(12668953239018839444)
XLA Ops:
  0.6 14.7 %shard_map.95 = (bf16[16,4,4,128]{3,2,1,0:T(4,128)(2,1)S(1)}, f32[4,256]{1,0:T(4,128)S(1)}) custom-call(bf16[4,64,128]{2,1,0:T(8,128)(2,1)} %query_hbm.1, bf16[4,64,128]{2,1,0:T(8,128)(2,1)} %key_hbm.1, bf16[4,64,128]{2,1,0:T(8,128)(2,1)} %value_hbm.1, bf16[4,64,128]{2,1,0:T(8,128)(2,1)} %out_hbm.1, bf16[4,64,128]{2,1,0:T(8,128)(2,1)} %grad_hbm.1, ...), custom_call_target="tpu_custom_call" | custom-call | tf_op jit(solution)/shard_map/pallas_call | solution.py:267
  15.4 0.7 %shard_map.96 = (bf16[4,64,128]{2,1,0:T(8,128)(2,1)}, f32[4,4,64]{2,1,0:T(4,128)}) custom-call(bf16[16,4,4,128]{3,2,1,0:T(4,128)(2,1)S(1)} %get-tuple-element.4.pairs, f32[4,256]{1,0:T(4,128)S(1)} %get-tuple-element.5.total), custom_call_target="tpu_custom_call" | custom-call | tf_op jit(solution)/shard_map/pallas_call | solution.py:301
